TPU v7x, 128 devices: a whole 4x4x4 slice. The times are simulated.
128 devices in a mesh: slot: 32 (over y, x, core), own: 4 (over z).
Axes of the slice: x: 4, y: 4, z: 4, core: 2. Of those that a mesh axis runs over, the one named last changes fastest.
Arguments:
- slot_grads: bfloat16 [128, 768, 2048], P(('slot', 'own')), may hold values from -6 to 6
- weights: bfloat16 [64, 768, 2048], P(None, 'slot', 'own'), may hold values from -0.21875 to 0.21875
- moment: float32 [64, 768, 2048], P(None, 'slot', 'own'), may hold values from -2 to 2
- second: float32 [64, 768, 2048], P(None, 'slot', 'own'), may hold values from 0.01 to 1
- counts_old: int32 [64], replicated, may hold values from 1 to 4, as said below
- counts_new: int32 [64], replicated, may hold values from 1 to 4, as said below
- inputs: bfloat16 [32768, 768], P(('slot', 'own')), may hold values from -6 to 6
- row_slot: int32 [32768, 1], P(('slot', 'own')), may hold values from 0 to 127; in each aligned block of 256 rows (0 to 255, 256 to 511, ...) at most 4 rows name the same one
Outputs:
- new_weights: bfloat16 [64, 768, 2048], P(None, 'slot', 'own')
- new_moment: float32 [64, 768, 2048], P(None, 'slot', 'own')
- new_second: float32 [64, 768, 2048], P(None, 'slot', 'own')
- outputs: bfloat16 [32768, 2048], P(('slot', 'own'))
Inputs may be any that keep to these rules, and one draw needn't show every extreme that they name: counts_old sums to 128; some expert has 4 replicas and some has 1. counts_new sums to 128; some expert has 4 replicas and some has 1. `row_slot`: the 256 rows of one device name any one slot at most 4 times, a bound that some block reaches.
All inputs are finite; a program needn't handle non-finite values.
Results may differ from a plain program's by a relative error of at most 0.0049.
Values may be sent and summed in bfloat16 or wider, within the bound.
No kernel may reach another device: no remote copies, remote signals or barrier semaphores. Data moves between devices by JAX's collectives and lax.ppermute only.
A program may use at most 128 MiB of HBM per device.

v0:
```python
import jax
import jax.numpy as jnp
from jax import lax
from jax.sharding import PartitionSpec as P


def slot_table(counts, n_slots):
    bounds = jnp.cumsum(counts)
    slots = jnp.arange(n_slots, dtype=jnp.int32)
    return jnp.sum((bounds[None, :] <= slots[:, None]).astype(jnp.int32), axis=1)


def body(slot_grads, weights, moment, second, counts_old, counts_new, inputs, row_slot):
    n_slot = lax.axis_size("slot")
    n_own = lax.axis_size("own")
    devices = n_slot * n_own
    experts, rows_here, cols_here = weights.shape
    width = slot_grads.shape[2]
    hidden = slot_grads.shape[1]
    tok_rows = inputs.shape[0]
    capacity = 2 * tok_rows // devices
    table_old = slot_table(counts_old, devices)
    table_new = slot_table(counts_new, devices)
    target = row_slot[:, 0]
    marks = (target[:, None] == jnp.arange(devices, dtype=jnp.int32)[None, :]).astype(jnp.int32)
    before = jnp.cumsum(marks, axis=0) - marks
    rank = jnp.sum(before * marks, axis=1)
    position = target * capacity + rank
    outgoing = jnp.zeros((devices * capacity, hidden), jnp.bfloat16).at[position].set(inputs)
    arrived = lax.all_to_all(
        outgoing.reshape(devices, capacity, hidden),
        ("slot", "own"),
        split_axis=0,
        concat_axis=0,
        tiled=True,
    )
    arrived = arrived.reshape(devices * capacity, hidden)
    sectioned = (
        slot_grads.reshape(n_slot, rows_here, n_own, cols_here)
        .transpose(0, 2, 1, 3)
        .reshape(devices, rows_here, cols_here)
    )
    pieces = lax.all_to_all(sectioned, ("slot", "own"), split_axis=0, concat_axis=0, tiled=True)
    source = jnp.arange(devices, dtype=jnp.int32)
    owner_of = table_old[source]
    select = (owner_of[None, :] == jnp.arange(experts, dtype=jnp.int32)[:, None]).astype(
        jnp.bfloat16
    )
    grads = jnp.dot(
        select, pieces.reshape(devices, rows_here * cols_here), preferred_element_type=jnp.float32
    ).reshape(experts, rows_here, cols_here)
    new_moment = 0.9 * moment + 0.1 * grads
    new_second = 0.95 * second + 0.05 * grads * grads
    bias_one = 1.0 - 0.9**10
    bias_two = 1.0 - 0.95**10
    update = 0.001 * (new_moment / bias_one) / (jnp.sqrt(new_second / bias_two) + 1e-08)
    new_weights = (weights.astype(jnp.float32) - update).astype(jnp.bfloat16)
    hosted = new_weights[table_new]
    landed = lax.all_to_all(hosted, ("slot", "own"), split_axis=0, concat_axis=0, tiled=True)
    slot_weight = (
        landed.reshape(n_slot, n_own, rows_here, cols_here)
        .transpose(0, 2, 1, 3)
        .reshape(hidden, width)
    )
    produced = jnp.dot(arrived, slot_weight, preferred_element_type=jnp.float32).astype(
        jnp.bfloat16
    )
    returned = lax.all_to_all(
        produced.reshape(devices, capacity, width),
        ("slot", "own"),
        split_axis=0,
        concat_axis=0,
        tiled=True,
    )
    outputs = returned.reshape(devices * capacity, width)[position]
    return (new_weights, new_moment, new_second, outputs)


def solution(mesh):
    placed = (
        P(("slot", "own"), None, None),
        P(None, "slot", "own"),
        P(None, "slot", "own"),
        P(None, "slot", "own"),
        P(),
        P(),
        P(("slot", "own"), None),
        P(("slot", "own"), None),
    )
    return jax.shard_map(
        body,
        mesh=mesh,
        in_specs=placed,
        out_specs=(
            P(None, "slot", "own"),
            P(None, "slot", "own"),
            P(None, "slot", "own"),
            P(("slot", "own"), None),
        ),
        check_vma=False,
    )
```

profile of v0, /device:TPU:1, one launch (start us, length us, event | category | flops | bytes accessed | tf_op | source)
XLA Modules:
  0.0 183.6 jit_solution(13248790534847788096)
XLA Ops:
  0.6 4.8 %reshape.118 = bf16[32,24,4,512]{3,2,1,0:T(4,128)(2,1)S(1)} reshape(bf16[1,768,2048]{2,1,0:T(8,128)(2,1)} %param.8) | data formatting | bytes 6291456 | tf_op jit(solution)/shard_map/reshape | solution.py:39
  5.4 2.6 %copy.51 = bf16[32,4,24,512]{3,2,1,0:T(8,128)(2,1)} copy(bf16[32,4,24,512]{3,1,2,0:T(4,128)(2,1)S(1)} %bitcast.49) | data formatting | bytes 6291456 | tf_op jit(solution)/shard_map/transpose | solution.py:40
  8.0 11.5 %all-to-all-start = ((bf16[128,24,512]{2,1,0:T(8,128)(2,1)}), bf16[128,24,512]{2,1,0:T(8,128)(2,1)S(1)}, u32[]{:S(2)}, u32[]{:S(2)}) async-start(bf16[128,24,512]{2,1,0:T(8,128)(2,1)} %bitcast.46), calls=%async_computation | async-start | bytes 6291456 | tf_op jit(solution)/shard_map/all_to_all | solution.py:43
  20.8 3.0 %scatter_custom_fusion = bf16[512,768]{1,0:T(8,128)(2,1)} fusion(s32[256]{0:T(256)S(1)} %bitcast.57, bf16[256,768]{1,0:T(8,128)(2,1)} %param.14, bf16[]{:T(256)} %constant.36.clone.1), kind=kCustom, calls=%fused_computation.13 | custom fusion | bytes 786944 | tf_op jit(solution)/shard_map/scatter | solution.py:29
  23.8 2.4 %reshape.122 = bf16[128,4,768]{2,1,0:T(4,128)(2,1)} reshape(bf16[512,768]{1,0:T(8,128)(2,1)} %scatter_custom_fusion) | data formatting | bytes 1572864 | tf_op jit(solution)/shard_map/reshape | solution.py:31
  26.3 1.2 gather_fusion
  27.6 33.6 %all-to-all-done = bf16[128,24,512]{2,1,0:T(8,128)(2,1)S(1)} async-done(((bf16[128,24,512]{2,1,0:T(8,128)(2,1)}), bf16[128,24,512]{2,1,0:T(8,128)(2,1)S(1)}, u32[]{:S(2)}, u32[]{:S(2)}) %all-to-all-start) | async-done | bytes 3145760 | tf_op jit(solution)/shard_map/all_to_all | solution.py:43
  61.2 4.6 %all-to-all-start.1 = ((bf16[128,4,768]{2,1,0:T(4,128)(2,1)}), bf16[128,4,768]{2,1,0:T(4,128)(2,1)}, u32[]{:S(2)}, u32[]{:S(2)}) async-start(bf16[128,4,768]{2,1,0:T(4,128)(2,1)} %reshape.122), calls=%async_computation.1 | async-start | bytes 1572864 | tf_op jit(solution)/shard_map/all_to_all | solution.py:30
  65.8 3.4 %copy.62 = bf16[128,24,512]{0,2,1:T(8,128)(2,1)} copy(bf16[128,24,512]{2,1,0:T(8,128)(2,1)S(1)} %all-to-all-done) | data formatting | bytes 6291456 | tf_op jit(solution)/shard_map/reshape | solution.py:50
  69.3 12.5 %subtract_convert_fusion = (bf16[64,24,512]{2,0,1:T(8,128)(2,1)S(1)}, f32[64,24,512]{2,0,1:T(8,128)}, f32[64,24,512]{2,0,1:T(8,128)}) fusion(bf16[64,24,512]{2,1,0:T(8,128)(2,1)} %param.9, f32[64,24,512]{2,1,0:T(8,128)} %param.10, f32[64,24,512]{2,1,0:T(8,128)} %param.11, bf16[128,24,512]{0,2,1:T(8,128)(2,1)} %copy.62, s32[128]{0:T(128)S(1)} %gather_fusion), kind=kOutput, calls=%fused_computation.11 | convolution fusion | flops 212344832 | bytes 18874880 | tf_op jit(solution)/shard_map/dot_general | solution.py:49
  82.7 2.4 %gather_fusion.1 = bf16[128,24,512]{2,1,0:T(8,128)(2,1)} fusion(bf16[64,24,512]{2,1,0:T(8,128)(2,1)S(1)} %copy.59, s32[1024]{0:T(1024)S(1)} %pad_clamp_fusion.1), kind=kCustom, calls=%fused_computation.1 | custom fusion | bytes 6291968 | tf_op jit(solution)/shard_map/gather | solution.py:58
  85.1 9.8 %all-to-all-start.2 = ((bf16[128,24,512]{2,1,0:T(8,128)(2,1)}), bf16[128,24,512]{2,1,0:T(8,128)(2,1)S(1)}, u32[]{:S(2)}, u32[]{:S(2)}) async-start(bf16[128,24,512]{2,1,0:T(8,128)(2,1)} %gather_fusion.1), calls=%async_computation.2 | async-start | bytes 6291456 | tf_op jit(solution)/shard_map/all_to_all | solution.py:59
  94.9 2.3 %reshape.123 = bf16[512,768]{1,0:T(8,128)(2,1)} reshape(bf16[128,4,768]{2,1,0:T(4,128)(2,1)} %all-to-all-done.1) | data formatting | bytes 1572864 | tf_op jit(solution)/shard_map/reshape | solution.py:37
  97.2 39.4 %all-to-all-done.2 = bf16[128,24,512]{2,1,0:T(8,128)(2,1)S(1)} async-done(((bf16[128,24,512]{2,1,0:T(8,128)(2,1)}), bf16[128,24,512]{2,1,0:T(8,128)(2,1)S(1)}, u32[]{:S(2)}, u32[]{:S(2)}) %all-to-all-start.2) | async-done | bytes 3145760 | tf_op jit(solution)/shard_map/all_to_all | solution.py:59
  136.6 1.6 copy.58
  138.3 1.0 copy.63
  139.4 1.8 convolution_convert_fusion
  141.2 2.2 %reshape.128 = bf16[128,4,2048]{2,1,0:T(4,128)(2,1)} reshape(bf16[512,2048]{1,0:T(8,128)(2,1)S(1)} %convolution_convert_fusion) | data formatting | bytes 4194304 | tf_op jit(solution)/shard_map/reshape | solution.py:69
  143.4 5.0 %all-to-all-start.3 = ((bf16[128,4,2048]{2,1,0:T(4,128)(2,1)}), bf16[128,4,2048]{2,1,0:T(4,128)(2,1)}, u32[]{:S(2)}, u32[]{:S(2)}) async-start(bf16[128,4,2048]{2,1,0:T(4,128)(2,1)} %reshape.128), calls=%async_computation.3 | async-start | bytes 4194304 | tf_op jit(solution)/shard_map/all_to_all | solution.py:68
  148.5 3.5 %copy.60 = f32[64,24,512]{2,1,0:T(8,128)} copy(f32[64,24,512]{2,0,1:T(8,128)S(1)} %copy-done.2) | data formatting | bytes 6291456
  152.0 3.5 %copy.61 = f32[64,24,512]{2,1,0:T(8,128)} copy(f32[64,24,512]{2,0,1:T(8,128)S(1)} %copy-done.1) | data formatting | bytes 6291456
  155.5 23.2 %all-to-all-done.3 = bf16[128,4,2048]{2,1,0:T(4,128)(2,1)} async-done(((bf16[128,4,2048]{2,1,0:T(4,128)(2,1)}), bf16[128,4,2048]{2,1,0:T(4,128)(2,1)}, u32[]{:S(2)}, u32[]{:S(2)}) %all-to-all-start.3) | async-done | bytes 2097184 | tf_op jit(solution)/shard_map/all_to_all | solution.py:68
  178.7 2.5 %reshape.129 = bf16[512,2048]{1,0:T(8,128)(2,1)S(1)} reshape(bf16[128,4,2048]{2,1,0:T(4,128)(2,1)} %all-to-all-done.3) | data formatting | bytes 4194304 | tf_op jit(solution)/shard_map/reshape | solution.py:75
  181.2 2.3 %gather_fusion.2 = bf16[256,2048]{1,0:T(8,128)(2,1)} fusion(bf16[512,2048]{1,0:T(8,128)(2,1)S(1)} %reshape.129, s32[1024]{0:T(1024)S(1)} %pad_clamp_fusion), kind=kCustom, calls=%fused_computation.2 | custom fusion | bytes 2098176 | tf_op jit(solution)/shard_map/gather | solution.py:75
  (39 shorter events, 2.4 us)
Async XLA Ops:
  8.0 11.5 %copy-start.5 = (s32[64]{0:T(128)S(1)}, s32[64]{0:T(128)}, u32[]{:S(2)}) copy-start(s32[64]{0:T(128)} %param.12) | copy-start | bytes 772
  8.0 11.8 %copy-start.6 = (s32[64]{0:T(128)S(1)}, s32[64]{0:T(128)}, u32[]{:S(2)}) copy-start(s32[64]{0:T(128)} %param.13) | copy-start | bytes 772
  8.0 12.1 %copy-start.4 = (s32[256,1]{0,1:T(1,128)S(1)}, s32[256,1]{0,1:T(1,128)}, u32[]{:S(2)}) copy-start(s32[256,1]{0,1:T(1,128)} %param.15) | copy-start | bytes 3076
  8.0 53.2 %all-to-all-start = ((bf16[128,24,512]{2,1,0:T(8,128)(2,1)}), bf16[128,24,512]{2,1,0:T(8,128)(2,1)S(1)}, u32[]{:S(2)}, u32[]{:S(2)}) async-start(bf16[128,24,512]{2,1,0:T(8,128)(2,1)} %bitcast.46), calls=%async_computation | async-start | bytes 6291456 | tf_op jit(solution)/shard_map/all_to_all | solution.py:43
  61.2 23.9 %all-to-all-start.1 = ((bf16[128,4,768]{2,1,0:T(4,128)(2,1)}), bf16[128,4,768]{2,1,0:T(4,128)(2,1)}, u32[]{:S(2)}, u32[]{:S(2)}) async-start(bf16[128,4,768]{2,1,0:T(4,128)(2,1)} %reshape.122), calls=%async_computation.1 | async-start | bytes 1572864 | tf_op jit(solution)/shard_map/all_to_all | solution.py:30
  82.7 2.4 %copy-start = (bf16[64,24,512]{2,1,0:T(8,128)(2,1)}, bf16[64,24,512]{2,1,0:T(8,128)(2,1)S(1)}, u32[]{:S(2)}) copy-start(bf16[64,24,512]{2,1,0:T(8,128)(2,1)S(1)} %copy.59) | copy-start | bytes 4718596
  85.1 51.5 %all-to-all-start.2 = ((bf16[128,24,512]{2,1,0:T(8,128)(2,1)}), bf16[128,24,512]{2,1,0:T(8,128)(2,1)S(1)}, u32[]{:S(2)}, u32[]{:S(2)}) async-start(bf16[128,24,512]{2,1,0:T(8,128)(2,1)} %gather_fusion.1), calls=%async_computation.2 | async-start | bytes 6291456 | tf_op jit(solution)/shard_map/all_to_all | solution.py:59
  138.2 1.1 copy-start.3
  143.4 5.0 %copy-start.2 = (f32[64,24,512]{2,0,1:T(8,128)S(1)}, f32[64,24,512]{2,0,1:T(8,128)}, u32[]{:S(2)}) copy-start(f32[64,24,512]{2,0,1:T(8,128)} %get-tuple-element.21) | copy-start | bytes 9437188
  143.4 35.3 %all-to-all-start.3 = ((bf16[128,4,2048]{2,1,0:T(4,128)(2,1)}), bf16[128,4,2048]{2,1,0:T(4,128)(2,1)}, u32[]{:S(2)}, u32[]{:S(2)}) async-start(bf16[128,4,2048]{2,1,0:T(4,128)(2,1)} %reshape.128), calls=%async_computation.3 | async-start | bytes 4194304 | tf_op jit(solution)/shard_map/all_to_all | solution.py:68
  148.5 3.5 %copy-start.1 = (f32[64,24,512]{2,0,1:T(8,128)S(1)}, f32[64,24,512]{2,0,1:T(8,128)}, u32[]{:S(2)}) copy-start(f32[64,24,512]{2,0,1:T(8,128)} %get-tuple-element.22) | copy-start | bytes 9437188
where the time goes:
time: 184 us
  waiting for transfers between devices  96.2 us (52%)
  local copies, waits for them, and re-layouts  40.2 us (22%)
  starting transfers between devices  31 us (17%)
  matrix products  14.3 us (8%)
    all_to_all x1, waiting for transfers between devices, body(): lax.all_to_all(hosted, ('slot', 'own'), split_axis=0, concat_axis=0, tile...  39.4 us
    all_to_all x1, waiting for transfers between devices, body(): lax.all_to_all(sectioned, ('slot', 'own'), split_axis=0, concat_axis=0, t...  33.6 us
    all_to_all x1, waiting for transfers between devices, body(): lax.all_to_all(produced.reshape(devices, capacity, width), ('slot', 'own'...  23.2 us
    dot_general x1, matrix products, body(): jnp.dot(select, pieces.reshape(devices, rows_here * cols_here), preferred...  12.5 us
    all_to_all x1, starting transfers between devices, body(): lax.all_to_all(sectioned, ('slot', 'own'), split_axis=0, concat_axis=0, t...  11.5 us
    all_to_all x1, starting transfers between devices, body(): lax.all_to_all(hosted, ('slot', 'own'), split_axis=0, concat_axis=0, tile...  9.84 us
    unnamed x19, local copies, waits for them, and re-layouts  9 us
    all_to_all x1, starting transfers between devices, body(): lax.all_to_all(produced.reshape(devices, capacity, width), ('slot', 'own'...  5.02 us
  transfers between devices with their start and end apart: 4, of which 3 were waited for; matrix products, arithmetic and copies ran while one was open for 20% of the time, Pallas kernels for 0%

commit v1 on v0

v1 whole, which is shorter than its diff:
```python
import jax
import jax.numpy as jnp
from jax import lax
from jax.experimental import pallas as pl
from jax.experimental.pallas import tpu as pltpu
from jax.sharding import PartitionSpec as P

ALL = ("slot", "own")
F32 = jnp.float32
BF16 = jnp.bfloat16
MIB = 1 << 20


def exchange(array):
    return lax.all_to_all(array, ALL, split_axis=0, concat_axis=0, tiled=True)


def rank_column(target):
    rows = target.shape[0]
    at = lax.broadcasted_iota(jnp.int32, (rows, rows), 0)
    to = lax.broadcasted_iota(jnp.int32, (rows, rows), 1)
    across = jnp.sum(jnp.where(at == to, target, 0), axis=0, keepdims=True)
    same = target == across
    return at, to, across, same


def pack_kernel(slot_ref, grads_ref, inputs_ref, out_ref, place_ref, *, groups, owners, hidden_rows, wide):
    parts = hidden_rows // 8

    @pl.when(pl.program_id(0) == 0)
    def _():
        target = slot_ref[...]
        at, to, across, same = rank_column(target)
        rank = jnp.sum(jnp.where(same & (at < to), 1, 0), axis=0, keepdims=True)
        place_ref[...] = jnp.broadcast_to(across * 8 + rank, place_ref.shape)

    for q in range(groups):
        for z in range(owners):
            for i in range(parts):
                out_ref[q * owners + z, :, i * wide : (i + 1) * wide] = grads_ref[
                    0, pl.ds(q * hidden_rows + 8 * i, 8), z * wide : (z + 1) * wide
                ]
    there = groups * owners * 8
    half = inputs_ref.shape[1] // 2
    tokens = inputs_ref.shape[0]
    row = lax.broadcasted_iota(jnp.int32, (there, tokens), 0)
    line = pl.program_id(0) * there + row - (row & 4)
    chosen = jnp.where(line == place_ref[0:1, :], 1.0, 0.0).astype(BF16)
    low = jnp.dot(chosen, inputs_ref[:, :half], preferred_element_type=F32)
    high = jnp.dot(chosen, inputs_ref[:, half:], preferred_element_type=F32)
    upper = (lax.broadcasted_iota(jnp.int32, (there, half), 0) & 4) > 0
    rows = jnp.where(upper, high, low).reshape(groups * owners, 8, half)
    out_ref[:, :, parts * wide :] = rows.astype(BF16)


def adam_kernel(
    table_ref, pieces_ref, weights_ref, moment_ref, second_ref, nw_ref, nm_ref, nv_ref, hosted_ref, *, block, wide
):
    parts = weights_ref.shape[1] // 8
    last = pieces_ref.shape[0] - 1
    bias_one = 1.0 - 0.9**10
    bias_two = 1.0 - 0.95**10
    base = pl.program_id(0) * block

    def one(k, carry):
        e = base + k
        start = table_ref[0, e]
        count = table_ref[1, e]
        start_new = table_ref[2, e]
        count_new = table_ref[3, e]
        for i in range(parts):
            cols = slice(i * wide, (i + 1) * wide)
            rows = slice(8 * i, 8 * i + 8)
            g = pieces_ref[start, :, cols].astype(F32)
            for j in range(1, 4):
                piece = pieces_ref[jnp.minimum(start + j, last), :, cols].astype(F32)
                g = g + jnp.where(count > j, piece, 0.0)
            nm = 0.9 * moment_ref[k, rows, :] + 0.1 * g
            nv = 0.95 * second_ref[k, rows, :] + 0.05 * g * g
            nm_ref[k, rows, :] = nm
            nv_ref[k, rows, :] = nv
            update = 0.001 * (nm / bias_one) / (jnp.sqrt(nv / bias_two) + 1e-08)
            nw = (weights_ref[k, rows, :].astype(F32) - update).astype(BF16)
            nw_ref[k, rows, :] = nw
            for j in range(4):

                @pl.when(j < count_new)
                def _():
                    hosted_ref[start_new + j, :, cols] = nw

        return carry

    lax.fori_loop(0, block, one, 0)


def lhs_kernel(rows_ref, lhs_ref):
    half = rows_ref.shape[2]
    wide = rows_ref[...].astype(F32).reshape(rows_ref.shape[0] // 2, 2, 8, half)
    even = wide[:, 0]
    odd = wide[:, 1]
    first = lax.broadcasted_iota(jnp.int32, even.shape, 1) < 4
    low = jnp.where(first, even, pltpu.roll(odd, 4, 1))
    high = jnp.where(first, pltpu.roll(even, 4, 1), odd)
    rows = even.shape[0] * 8
    lhs_ref[:, :half] = low.reshape(rows, half).astype(BF16)
    lhs_ref[:, half:] = high.reshape(rows, half).astype(BF16)


def product_kernel(landed_ref, lhs_ref, out_ref, matrix_ref, *, owners, wide, step):
    parts = landed_ref.shape[2] // wide
    groups = landed_ref.shape[0] // owners
    for s in range(groups):
        for z in range(owners):
            for i in range(parts):
                matrix_ref[(s * parts + i) * 8 : (s * parts + i) * 8 + 8, z * wide : (z + 1) * wide] = landed_ref[
                    s * owners + z, :, i * wide : (i + 1) * wide
                ]
    half = matrix_ref.shape[1] // 2
    devices = out_ref.shape[0]
    lhs = lhs_ref[...]
    for n in range(0, half, step):
        a = jnp.dot(lhs, matrix_ref[:, n : n + step], preferred_element_type=F32)
        b = jnp.dot(lhs, matrix_ref[:, half + n : half + n + step], preferred_element_type=F32)
        a = a.reshape(devices // 2, 8, step)
        b = b.reshape(devices // 2, 8, step)
        first = lax.broadcasted_iota(jnp.int32, a.shape, 1) < 4
        even = jnp.where(first, a, pltpu.roll(b, 4, 1)).astype(BF16)
        odd = jnp.where(first, pltpu.roll(a, 4, 1), b).astype(BF16)
        out_ref[:, :, n : n + step] = jnp.stack([even, odd], axis=1).reshape(devices, 8, step)


def gather_kernel(slot_ref, returned_ref, out_ref):
    target = slot_ref[...]
    at, to, _, same = rank_column(target)
    rank = jnp.sum(jnp.where(same & (to < at), 1, 0), axis=1, keepdims=True)
    place = target * 8 + rank
    tokens = target.shape[0]
    lines, half = returned_ref.shape
    column = lax.broadcasted_iota(jnp.int32, (tokens, lines), 1)
    for h in range(2):
        chosen = jnp.where(column == place + 4 * h, 1.0, 0.0).astype(BF16)
        out_ref[:, h * half : (h + 1) * half] = jnp.dot(
            chosen, returned_ref[...], preferred_element_type=F32
        ).astype(BF16)


def params(mib=48):
    return pltpu.CompilerParams(vmem_limit_bytes=mib * MIB)


def body(slot_grads, weights, moment, second, counts_old, counts_new, inputs, row_slot):
    owners = lax.axis_size("own")
    devices = lax.axis_size("slot") * owners
    experts, rows_here, cols_here = weights.shape
    hidden, width = slot_grads.shape[1:]
    tokens = inputs.shape[0]
    parts = rows_here // 8
    half = hidden // 2
    span = parts * cols_here
    whole = lambda *shape: pl.BlockSpec(shape, lambda *_: (0,) * len(shape))

    steps = 8
    groups = devices // owners // steps
    packed = pl.pallas_call(
        lambda *refs: pack_kernel(*refs, groups=groups, owners=owners, hidden_rows=rows_here, wide=cols_here),
        out_shape=jax.ShapeDtypeStruct((devices, 8, span + half), BF16),
        grid=(steps,),
        in_specs=[
            whole(tokens, 1),
            pl.BlockSpec((1, groups * rows_here, width), lambda k: (0, k, 0)),
            whole(tokens, hidden),
        ],
        out_specs=pl.BlockSpec((groups * owners, 8, span + half), lambda k: (k, 0, 0)),
        scratch_shapes=[pltpu.VMEM((8, tokens), jnp.int32)],
        compiler_params=params(),
        name="pack",
    )(row_slot, slot_grads, inputs)
    arrived = exchange(packed)

    table = jnp.stack(
        [jnp.cumsum(counts_old) - counts_old, counts_old, jnp.cumsum(counts_new) - counts_new, counts_new]
    ).astype(jnp.int32)
    block = 8
    state = pl.BlockSpec((block, rows_here, cols_here), lambda k, *_: (k, 0, 0))
    new_weights, new_moment, new_second, hosted = pl.pallas_call(
        lambda *refs: adam_kernel(*refs, block=block, wide=cols_here),
        out_shape=(
            jax.ShapeDtypeStruct(weights.shape, BF16),
            jax.ShapeDtypeStruct(moment.shape, F32),
            jax.ShapeDtypeStruct(second.shape, F32),
            jax.ShapeDtypeStruct((devices, 8, span), BF16),
        ),
        grid_spec=pltpu.PrefetchScalarGridSpec(
            num_scalar_prefetch=1,
            grid=(experts // block,),
            in_specs=[whole(devices, 8, span), state, state, state],
            out_specs=(state, state, state, whole(devices, 8, span)),
        ),
        compiler_params=params(),
        name="adam",
    )(table, arrived, weights, moment, second)
    landed = exchange(hosted)

    lhs = pl.pallas_call(
        lhs_kernel,
        out_shape=jax.ShapeDtypeStruct((devices * 4, hidden), BF16),
        grid=(1,),
        in_specs=[pl.BlockSpec((devices, 8, half), lambda k: (0, 0, span // half))],
        out_specs=whole(devices * 4, hidden),
        compiler_params=params(),
        name="lhs",
    )(arrived)
    produced = pl.pallas_call(
        lambda *refs: product_kernel(*refs, owners=owners, wide=cols_here, step=256),
        out_shape=jax.ShapeDtypeStruct((devices, 8, width // 2), BF16),
        grid=(1,),
        in_specs=[whole(devices, 8, span), whole(devices * 4, hidden)],
        out_specs=whole(devices, 8, width // 2),
        scratch_shapes=[pltpu.VMEM((hidden, width), BF16)],
        compiler_params=params(),
        name="product",
    )(landed, lhs)
    returned = exchange(produced)

    outputs = pl.pallas_call(
        gather_kernel,
        out_shape=jax.ShapeDtypeStruct((tokens, width), BF16),
        grid=(1,),
        in_specs=[whole(tokens, 1), whole(devices * 8, width // 2)],
        out_specs=whole(tokens, width),
        compiler_params=params(),
        name="gather",
    )(row_slot, returned.reshape(devices * 8, width // 2))
    return (new_weights, new_moment, new_second, outputs)


def solution(mesh):
    placed = (
        P(ALL, None, None),
        P(None, "slot", "own"),
        P(None, "slot", "own"),
        P(None, "slot", "own"),
        P(),
        P(),
        P(ALL, None),
        P(ALL, None),
    )
    return jax.shard_map(
        body,
        mesh=mesh,
        in_specs=placed,
        out_specs=(
            P(None, "slot", "own"),
            P(None, "slot", "own"),
            P(None, "slot", "own"),
            P(ALL, None),
        ),
        check_vma=False,
    )
```

time: 184 us -> 172 us (0.935)
  blocking collectives: 0 us -> 34.1 us
  local copies, waits for them, and re-layouts: 40.2 us -> 7.57 us
  Pallas kernels: 0 us -> 23.9 us
  starting transfers between devices: 31 us -> 16.2 us
  matrix products: 14.3 us -> 0 us
  waiting for transfers between devices: 96.2 us -> 88.8 us
    all_to_all x0 -> x1, blocking collectives: none -> 34.1 us  [exchange(): return lax.all_to_all(array, ALL, split_axis=0, concat_axis=0, tiled=True)]
    pallas_call x0 -> x5, Pallas kernels: none -> 23.9 us  [the longest x1 13.7 us: body(): pl.pallas_call(lambda *refs: adam_kernel(*refs, block=block, wide=cols_he...]
    reshape x7 -> x0, local copies, waits for them, and re-layouts: 19.2 us -> none  [the longest x1 4.79 us: body(): slot_grads.reshape(n_slot, rows_here, n_own, cols_here)]
    all_to_all x4 -> x2, starting transfers between devices: 31 us -> 16.2 us  [exchange(): return lax.all_to_all(array, ALL, split_axis=0, concat_axis=0, tiled=True)]
    dot_general x2 -> x0, matrix products: 14.3 us -> none  [the longest x1 12.5 us: body(): jnp.dot(select, pieces.reshape(devices, rows_here * cols_here), preferred...]
    all_to_all x4 -> x2, waiting for transfers between devices: 96.2 us -> 88.8 us  [exchange(): return lax.all_to_all(array, ALL, split_axis=0, concat_axis=0, tiled=True)]
    gather x3 -> x0, local copies, waits for them, and re-layouts: 5.97 us -> none  [the longest x1 2.41 us: body(): hosted = new_weights[table_new]]
    scatter x1 -> x0, local copies, waits for them, and re-layouts: 3.04 us -> none  [body(): jnp.zeros((devices * capacity, hidden), jnp.bfloat16).at[position]]
  transfers between devices with their start and end apart: 4 -> 2, of which waited for: 3 -> 2; matrix products, arithmetic and copies ran while one was open for 20% -> 0% of each run, Pallas kernels for 0% -> 1%
where the time goes in v1:
time: 172 us
  waiting for transfers between devices  88.8 us (52%)
  blocking collectives  34.1 us (20%)
  Pallas kernels  23.9 us (14%)
  starting transfers between devices  16.2 us (9%)
  local copies, waits for them, and re-layouts  7.57 us (4%)
    all_to_all x2, waiting for transfers between devices, exchange(): return lax.all_to_all(array, ALL, split_axis=0, concat_axis=0, tiled=True)  88.8 us
    all_to_all x1, blocking collectives, exchange(): return lax.all_to_all(array, ALL, split_axis=0, concat_axis=0, tiled=True)  34.1 us
    all_to_all x2, starting transfers between devices, exchange(): return lax.all_to_all(array, ALL, split_axis=0, concat_axis=0, tiled=True)  16.2 us
    pallas_call x1, Pallas kernels, body(): pl.pallas_call(lambda *refs: adam_kernel(*refs, block=block, wide=cols_he...  13.7 us
    unnamed x17, local copies, waits for them, and re-layouts  7.38 us
    pallas_call x1, Pallas kernels, body(): pl.pallas_call(lambda *refs: pack_kernel(*refs, groups=groups, owners=own...  4.48 us
  transfers between devices with their start and end apart: 2, of which 2 were waited for; matrix products, arithmetic and copies ran while one was open for 0% of the time, Pallas kernels for 1%

profile of v1, /device:TPU:1, one launch (start us, length us, event | category | flops | bytes accessed | tf_op | source)
XLA Modules:
  0.0 171.7 jit_solution(9447441864404612)
XLA Ops:
  0.6 0.8 copy.18.refs_0_.slot_ref
  1.4 0.0 copy-start.1
  1.5 1.9 %copy-done.1 = bf16[1,768,2048]{2,1,0:T(8,128)(2,1)S(1)} copy-done((bf16[1,768,2048]{2,1,0:T(8,128)(2,1)S(1)}, bf16[1,768,2048]{2,1,0:T(8,128)(2,1)}, u32[]{:S(2)}) %copy-start.1) | copy-done | bytes 3145752
  3.3 1.0 copy-done.5
  4.3 4.5 %pack.1 = bf16[128,8,1920]{2,1,0:T(8,128)(2,1)} custom-call(s32[256,1]{1,0:T(8,128)S(1)} %copy.18.refs_0_.slot_ref, bf16[1,768,2048]{2,1,0:T(8,128)(2,1)S(1)} %copy-done.1, bf16[256,768]{1,0:T(8,128)(2,1)S(1)} %copy-done.5), custom_call_target="tpu_custom_call" | custom-call | tf_op jit(solution)/shard_map/pack/pallas_call | solution.py:164
  8.8 11.9 %all-to-all-start = ((bf16[128,8,1920]{2,1,0:T(8,128)(2,1)}), bf16[128,8,1920]{2,1,0:T(8,128)(2,1)}, u32[]{:S(2)}, u32[]{:S(2)}) async-start(bf16[128,8,1920]{2,1,0:T(8,128)(2,1)} %pack.1), calls=%async_computation | async-start | bytes 7864320 | tf_op jit(solution)/shard_map/all_to_all | solution.py:15
  20.7 0.1 copy.17
  20.8 0.1 reduce-window.19
  20.9 0.1 reduce.1
  21.0 0.1 copy.16
  21.1 0.1 reduce-window.18
  21.2 0.1 reduce
  21.4 49.4 %all-to-all-done.refs_1_.rows_ref = bf16[128,8,1920]{2,1,0:T(8,128)(2,1)} async-done(((bf16[128,8,1920]{2,1,0:T(8,128)(2,1)}), bf16[128,8,1920]{2,1,0:T(8,128)(2,1)}, u32[]{:S(2)}, u32[]{:S(2)}) %all-to-all-start) | async-done | bytes 3932192 | tf_op jit(solution)/shard_map/all_to_all | solution.py:15
  70.8 13.7 %adam.1 = (bf16[64,24,512]{2,1,0:T(8,128)(2,1)}, f32[64,24,512]{2,1,0:T(8,128)}, f32[64,24,512]{2,1,0:T(8,128)}, bf16[128,8,1536]{2,1,0:T(8,128)(2,1)S(1)}) custom-call(s32[4,64]{1,0:T(4,128)S(1)} %pad_add_fusion.refs_0_, bf16[128,8,1920]{2,1,0:T(8,128)(2,1)} %all-to-all-done.refs_1_.rows_ref, bf16[64,24,512]{2,1,0:T(8,128)(2,1)S(1)} %copy-done.4, ...), custom_call_target="tpu_custom_call" | custom-call | tf_op jit(solution)/shard_map/adam/pallas_call | solution.py:185
  84.5 1.7 copy-done
  86.1 4.3 %all-to-all-start.1 = ((bf16[128,8,1536]{2,1,0:T(8,128)(2,1)}), bf16[128,8,1536]{2,1,0:T(8,128)(2,1)S(1)}, u32[]{:S(2)}, u32[]{:S(2)}) async-start(bf16[128,8,1536]{2,1,0:T(8,128)(2,1)} %copy-done), calls=%async_computation.1 | async-start | bytes 6291456 | tf_op jit(solution)/shard_map/all_to_all | solution.py:15
  90.4 1.4 lhs.3.refs_1_
  91.8 0.0 copy-start.2
  91.8 0.9 copy-done.2
  92.7 39.4 %all-to-all-done.1.refs_0_ = bf16[128,8,1536]{2,1,0:T(8,128)(2,1)S(1)} async-done(((bf16[128,8,1536]{2,1,0:T(8,128)(2,1)}), bf16[128,8,1536]{2,1,0:T(8,128)(2,1)S(1)}, u32[]{:S(2)}, u32[]{:S(2)}) %all-to-all-start.1) | async-done | bytes 3145760 | tf_op jit(solution)/shard_map/all_to_all | solution.py:15
  132.1 1.1 copy-done.3
  133.3 1.8 %product.1 = bf16[128,8,1024]{2,1,0:T(8,128)(2,1)S(1)} custom-call(bf16[128,8,1536]{2,1,0:T(8,128)(2,1)S(1)} %all-to-all-done.1.refs_0_, bf16[512,768]{1,0:T(8,128)(2,1)S(1)} %copy-done.3), custom_call_target="tpu_custom_call" | custom-call | tf_op jit(solution)/shard_map/product/pallas_call | solution.py:213
  135.1 34.1 %all_to_all.15 = bf16[128,8,1024]{2,1,0:T(8,128)(2,1)S(1)} all-to-all(bf16[128,8,1024]{2,1,0:T(8,128)(2,1)S(1)} %product.1), channel_id=1, replica_groups=mesh['slot'=32,'own'=4] {'slot','own'}, dimensions={0} | all-to-all | bytes 4194304 | tf_op jit(solution)/shard_map/all_to_all | solution.py:15
  169.2 2.5 %gather.1 = bf16[256,2048]{1,0:T(8,128)(2,1)} custom-call(s32[256,1]{1,0:T(8,128)S(1)} %copy.18.refs_0_.slot_ref, bf16[1024,1024]{1,0:T(8,128)(2,1)S(1)} %bitcast.9), custom_call_target="tpu_custom_call" | custom-call | tf_op jit(solution)/shard_map/gather/pallas_call | solution.py:225
  (11 shorter events, 0.0 us)
Async XLA Ops:
  1.4 1.9 %copy-start.1 = (bf16[1,768,2048]{2,1,0:T(8,128)(2,1)S(1)}, bf16[1,768,2048]{2,1,0:T(8,128)(2,1)}, u32[]{:S(2)}) copy-start(bf16[1,768,2048]{2,1,0:T(8,128)(2,1)} %refs_1_.1) | copy-start | bytes 9437188
  3.3 1.0 copy-start.5
  8.8 11.9 %copy-start.6 = (s32[64]{0:T(128)S(1)}, s32[64]{0:T(128)}, u32[]{:S(2)}) copy-start(s32[64]{0:T(128)} %param.13) | copy-start | bytes 772
  8.8 12.2 %copy-start.7 = (s32[64]{0:T(128)S(1)}, s32[64]{0:T(128)}, u32[]{:S(2)}) copy-start(s32[64]{0:T(128)} %param.12) | copy-start | bytes 772
  8.8 62.0 %copy-start.4 = (bf16[64,24,512]{2,1,0:T(8,128)(2,1)S(1)}, bf16[64,24,512]{2,1,0:T(8,128)(2,1)}, u32[]{:S(2)}) copy-start(bf16[64,24,512]{2,1,0:T(8,128)(2,1)} %refs_2_.3) | copy-start | bytes 4718596
  8.8 62.0 %all-to-all-start = ((bf16[128,8,1920]{2,1,0:T(8,128)(2,1)}), bf16[128,8,1920]{2,1,0:T(8,128)(2,1)}, u32[]{:S(2)}, u32[]{:S(2)}) async-start(bf16[128,8,1920]{2,1,0:T(8,128)(2,1)} %pack.1), calls=%async_computation | async-start | bytes 7864320 | tf_op jit(solution)/shard_map/all_to_all | solution.py:15
  84.5 1.7 copy-start
  86.1 46.0 %all-to-all-start.1 = ((bf16[128,8,1536]{2,1,0:T(8,128)(2,1)}), bf16[128,8,1536]{2,1,0:T(8,128)(2,1)S(1)}, u32[]{:S(2)}, u32[]{:S(2)}) async-start(bf16[128,8,1536]{2,1,0:T(8,128)(2,1)} %copy-done), calls=%async_computation.1 | async-start | bytes 6291456 | tf_op jit(solution)/shard_map/all_to_all | solution.py:15
  91.8 0.9 copy-start.2
  132.1 1.1 copy-start.3
